TPU v7x, 256 devices: a whole 4x4x8 slice. The times are simulated.
256 devices in a mesh: section: 32 (over x, z), expert: 8 (over y, core).
Axes of the slice: x: 4, y: 4, z: 8, core: 2. Of those that a mesh axis runs over, the one named last changes fastest.
Arguments:
- tokens: bfloat16 [2048, 4096], P('expert', 'section'), may hold values from -6 to 6
- routes: int32 [2048, 2], P('expert'), may hold values from 0 to 7, all different within a row; in each aligned block of 256 rows (0 to 255, 256 to 511, ...) at most 80 rows name the same one
- mix_weights: float32 [2048, 2], P('expert'), may hold values from 0.2 to 1
- w_gate: bfloat16 [8, 4096, 8192], P('expert', None, 'section'), may hold values from -0.1875 to 0.1875
- w_up: bfloat16 [8, 4096, 8192], P('expert', None, 'section'), may hold values from -0.1875 to 0.1875
- w_down: bfloat16 [8, 8192, 4096], P('expert', 'section'), may hold values from -0.125 to 0.125
- upstream: bfloat16 [2048, 4096], P('expert', 'section'), may hold values from -6 to 6
Outputs:
- mixed: bfloat16 [2048, 4096], P('expert', 'section')
- grad_tokens: bfloat16 [2048, 4096], P('expert', 'section')
- grad_mix: float32 [2048, 2], P('expert')
- grad_gate: bfloat16 [8, 4096, 8192], P('expert', None, 'section')
- grad_up: bfloat16 [8, 4096, 8192], P('expert', None, 'section')
- grad_down: bfloat16 [8, 8192, 4096], P('expert', 'section')
Inputs may be any that keep to these rules, and one draw needn't show every extreme that they name: `routes`: each token names 2 different experts. Among the 256 tokens of one index of the expert axis no expert is named more than 80 times, and in some such block one expert is named exactly 80 times.
All inputs are finite; a program needn't handle non-finite values.
Results may differ from a plain program's by a relative error of at most 0.02.
Values may be sent and summed in bfloat16 or wider, within the bound.
No kernel may reach another device: no remote copies, remote signals or barrier semaphores. Data moves between devices by JAX's collectives and lax.ppermute only.
A program may use at most 128 MiB of HBM per device.

v0:
```python
import jax
import jax.numpy as jnp
from jax import lax
from jax.sharding import PartitionSpec as P

highest = lax.Precision.HIGHEST


def slot_tables(route_rows, mix_rows, capacity, experts):
    tok_count, top_count = route_rows.shape
    flat_routes = route_rows.reshape(-1)
    onehot = (flat_routes[:, None] == jnp.arange(experts, dtype=jnp.int32)[None, :]).astype(
        jnp.int32
    )
    earlier = jnp.cumsum(onehot, axis=0) - onehot
    position = jnp.sum(earlier * onehot, axis=1)
    target = (flat_routes * capacity + position).reshape(tok_count, top_count)
    slot_ids = jnp.arange(experts * capacity, dtype=jnp.int32)
    hits = target[None, :, :] == slot_ids[:, None, None]
    matches = hits.astype(jnp.float32)
    select = jnp.sum(matches, axis=2)
    weighted = jnp.sum(matches * mix_rows[None, :, :], axis=2)
    token_ids = jnp.arange(tok_count, dtype=jnp.int32)
    slot_token = jnp.sum(jnp.sum(hits.astype(jnp.int32), axis=2) * token_ids[None, :], axis=1)
    return (target, select, weighted, slot_token)


def per_device(tokens, routes, mix_weights, w_gate, w_up, w_down, upstream):
    experts = lax.axis_size("expert")
    tok_count = tokens.shape[0]
    top_count = routes.shape[1]
    capacity = 5 * tok_count * top_count // (4 * experts)
    slot_total = experts * capacity
    target, select, weighted, slot_token = slot_tables(routes, mix_weights, capacity, experts)
    slot_fill = jnp.sum(select, axis=1)
    slot_scale = jnp.sum(weighted, axis=1)
    gate_local = w_gate[0]
    up_local = w_up[0]
    down_local = w_down[0]

    def collect(source, factor):
        taken = source[slot_token].astype(jnp.float32)
        return (taken * factor[:, None]).astype(jnp.bfloat16)

    def to_experts(source, factor):
        block = collect(source, factor)
        arrived = lax.all_to_all(
            block.reshape(experts, capacity, -1), "expert", split_axis=0, concat_axis=0, tiled=True
        )
        whole = lax.all_gather(arrived, "section", axis=2, tiled=True)
        return whole.reshape(slot_total, -1)

    def to_sources(partial_value):
        summed = lax.psum_scatter(
            partial_value.reshape(experts, capacity, -1).astype(jnp.bfloat16),
            "section",
            scatter_dimension=2,
            tiled=True,
        )
        back = lax.all_to_all(summed, "expert", split_axis=0, concat_axis=0, tiled=True)
        return back.reshape(slot_total, -1)

    dispatched = to_experts(tokens, slot_fill)
    act_gate = jnp.dot(dispatched, gate_local, preferred_element_type=jnp.float32)
    act_up = jnp.dot(dispatched, up_local, preferred_element_type=jnp.float32)
    sig = jax.nn.sigmoid(act_gate)
    silu_gate = act_gate * sig
    hidden = (silu_gate * act_up).astype(jnp.bfloat16)
    partial_value = jnp.dot(hidden, down_local, preferred_element_type=jnp.float32)
    returned = to_sources(partial_value).astype(jnp.float32)
    moe_out = jnp.dot(weighted.T, returned, precision=highest)
    mixed = (tokens.astype(jnp.float32) + moe_out).astype(jnp.bfloat16)
    picked = returned[target]
    upstream_wide = upstream.astype(jnp.float32)
    mix_terms = jnp.einsum("tkd,td->tk", picked, upstream_wide, precision=highest)
    grad_mix = lax.psum(mix_terms, "section")
    grad_rows = to_experts(upstream, slot_scale)
    grad_hidden = lax.dot_general(
        grad_rows, down_local, (((1,), (1,)), ((), ())), preferred_element_type=jnp.float32
    )
    grad_down = lax.dot_general(
        hidden, grad_rows, (((0,), (0,)), ((), ())), preferred_element_type=jnp.float32
    ).astype(jnp.bfloat16)
    dsilu = sig * (1.0 + act_gate * (1.0 - sig))
    grad_act_gate = (grad_hidden * act_up * dsilu).astype(jnp.bfloat16)
    grad_act_up = (grad_hidden * silu_gate).astype(jnp.bfloat16)
    grad_gate = lax.dot_general(
        dispatched, grad_act_gate, (((0,), (0,)), ((), ())), preferred_element_type=jnp.float32
    ).astype(jnp.bfloat16)
    grad_up = lax.dot_general(
        dispatched, grad_act_up, (((0,), (0,)), ((), ())), preferred_element_type=jnp.float32
    ).astype(jnp.bfloat16)
    first = lax.dot_general(
        grad_act_gate, gate_local, (((1,), (1,)), ((), ())), preferred_element_type=jnp.float32
    )
    second = lax.dot_general(
        grad_act_up, up_local, (((1,), (1,)), ((), ())), preferred_element_type=jnp.float32
    )
    back_rows = to_sources(first + second).astype(jnp.float32)
    grad_moe = jnp.dot(select.T, back_rows, precision=highest)
    grad_tokens = (upstream_wide + grad_moe).astype(jnp.bfloat16)
    return (mixed, grad_tokens, grad_mix, grad_gate[None], grad_up[None], grad_down[None])


def solution(mesh):
    return jax.shard_map(
        per_device,
        mesh=mesh,
        in_specs=(
            P("expert", "section"),
            P("expert", None),
            P("expert", None),
            P("expert", None, "section"),
            P("expert", None, "section"),
            P("expert", "section", None),
            P("expert", "section"),
        ),
        out_specs=(
            P("expert", "section"),
            P("expert", "section"),
            P("expert", None),
            P("expert", None, "section"),
            P("expert", None, "section"),
            P("expert", "section", None),
        ),
        check_vma=False,
    )
```

profile of v0, /device:TPU:8, one launch (start us, length us, event | category | flops | bytes accessed | tf_op | source)
XLA Modules:
  0.0 783.5 jit_solution(15971595313948356913)
XLA Ops:
  11.4 2.1 select_reduce_fusion
  15.7 10.3 %all_to_all.20 = bf16[8,80,128]{2,1,0:T(8,128)(2,1)} all-to-all(bf16[8,80,128]{2,1,0:T(8,128)(2,1)S(1)} %fusion.17), channel_id=1, replica_groups=mesh['section'=32,'expert'=8] {'expert'}, dimensions={0} | all-to-all | bytes 327680 | tf_op jit(solution)/shard_map/all_to_all | solution.py:47
  28.3 9.5 %all_to_all.21 = bf16[8,80,128]{2,1,0:T(8,128)(2,1)} all-to-all(bf16[8,80,128]{2,1,0:T(8,128)(2,1)S(1)} %fusion.16), channel_id=1, replica_groups=mesh['section'=32,'expert'=8] {'expert'}, dimensions={0} | all-to-all | bytes 327680 | tf_op jit(solution)/shard_map/all_to_all | solution.py:47
  37.9 77.2 %all-gather.3.cloned.1.call-done = bf16[8,80,4096]{2,1,0:T(8,128)(2,1)} async-done(((bf16[8,80,128]{2,1,0:T(8,128)(2,1)}), bf16[8,80,4096]{2,1,0:T(8,128)(2,1)}) %all-gather.3.cloned.1.call-update) | async-done | bytes 5242896 | tf_op jit(solution)/shard_map/all_gather | solution.py:50
  115.2 5.7 fusion.7
  120.8 2.4 fusion.11
  123.2 81.6 %all-gather.5.cloned.1.call-done = bf16[8,80,4096]{2,1,0:T(8,128)(2,1)} async-done(((bf16[8,80,128]{2,1,0:T(8,128)(2,1)}), bf16[8,80,4096]{2,1,0:T(8,128)(2,1)}) %all-gather.5.cloned.1.call-update) | async-done | bytes 5242896 | tf_op jit(solution)/shard_map/all_gather | solution.py:50
  204.7 5.4 multiply_convert_fusion
  210.1 3.9 convolution_convert_fusion
  214.0 11.2 %copy.36 = bf16[8,80,4096]{1,0,2:T(8,128)(2,1)} copy(bf16[8,80,4096]{2,1,0:T(8,128)(2,1)} %convolution_convert_fusion) | data formatting | bytes 10485760
  225.2 13.1 %reshape.124 = bf16[4096,640]{1,0:T(8,128)(2,1)} reshape(bf16[4096,8,80]{2,1,0:T(8,128)(2,1)} %bitcast.66) | data formatting | bytes 10485760
  239.8 2.7 fusion.9
  242.5 3.9 add_convert_fusion
  246.4 11.2 %copy.38 = bf16[8,80,4096]{1,0,2:T(8,128)(2,1)} copy(bf16[8,80,4096]{2,1,0:T(8,128)(2,1)} %bitcast.69) | data formatting | bytes 10485760
  257.6 13.1 %reshape.126 = bf16[4096,640]{1,0:T(8,128)(2,1)} reshape(bf16[4096,8,80]{2,1,0:T(8,128)(2,1)} %bitcast.67) | data formatting | bytes 10485760
  271.7 5.7 fusion.1
  277.4 5.8 fusion
  283.2 180.6 %reduce-scatter.7.cloned.1.call-done = bf16[128,640]{1,0:T(8,128)(2,1)} async-done(((bf16[4096,640]{1,0:T(8,128)(2,1)}), bf16[128,640]{1,0:T(8,128)(2,1)}) %reduce-scatter.7.cloned.1.call-update) | async-done | bytes 163856
  465.8 4.8 all-to-all-start.1
  470.6 5.8 fusion.2
  476.4 215.3 %reduce-scatter.9.cloned.1.call-done = bf16[128,640]{1,0:T(8,128)(2,1)} async-done(((bf16[4096,640]{1,0:T(8,128)(2,1)}), bf16[128,640]{1,0:T(8,128)(2,1)}) %reduce-scatter.9.cloned.1.call-update) | async-done | bytes 163856
  693.7 4.8 all-to-all-start.3
  700.3 72.8 %psum.7 = f32[256,2]{0,1:T(2,128)} all-reduce(f32[256,2]{0,1:T(2,128)S(1)} %bitcast.81), channel_id=1, replica_groups=mesh['section'=32,'expert'=8] {'section'}, use_global_device_ids=true, to_apply=%region_11.12 | all-reduce | flops 512 | bytes 4096 | tf_op jit(solution)/shard_map/psum | solution.py:76
  773.2 2.4 fusion.13
  (65 shorter events, 18.5 us)
Async XLA Ops:
  7.2 197.6 %copy-start = (bf16[1,256,4096]{2,1,0:T(8,128)(2,1)S(1)}, bf16[1,256,4096]{2,1,0:T(8,128)(2,1)}, u32[]{:S(2)}) copy-start(bf16[1,256,4096]{2,1,0:T(8,128)(2,1)} %param.12) | copy-start | bytes 6291460
  7.2 6.4 copy-start.2
  7.2 18.9 %copy-start.3 = (bf16[256,128]{1,0:T(8,128)(2,1)S(1)}, bf16[256,128]{1,0:T(8,128)(2,1)}, u32[]{:S(2)}) copy-start(bf16[256,128]{1,0:T(8,128)(2,1)} %param.13) | copy-start | bytes 196612
  7.2 108.0 %all-gather.3.cloned.1.call-start = ((), (), s32[]{:S(2)}) async-start(), calls=%async_computation.6 | async-start | bytes 5406720 | tf_op jit(solution)/shard_map/all_gather | solution.py:50
  26.0 178.7 %all-gather.5.cloned.1.call-start = ((), (), s32[]{:S(2)}) async-start(), calls=%async_computation.7 | async-start | bytes 5406720 | tf_op jit(solution)/shard_map/all_gather | solution.py:50
  37.9 425.9 %reduce-scatter.7.cloned.1.call-start = ((), (), s32[]{:S(2)}) async-start(), calls=%async_computation.8 | async-start | bytes 5406720
  115.2 5.7 copy-start.4
  115.2 5.7 copy-start.10
  238.2 1.6 copy-start.5
  238.3 453.4 %reduce-scatter.9.cloned.1.call-start = ((), (), s32[]{:S(2)}) async-start(), calls=%async_computation.9 | async-start | bytes 5406720
  239.8 2.7 copy-start.6
  239.8 2.7 copy-start.8
  270.7 1.0 copy-start.9
  271.7 5.7 copy-start.7
  465.8 227.9 %all-to-all-start.1 = ((bf16[8,80,128]{2,1,0:T(8,128)(2,1)}), bf16[8,80,128]{2,1,0:T(8,128)(2,1)S(1)}, u32[]{:S(2)}, u32[]{:S(2)}) async-start(bf16[8,80,128]{2,1,0:T(8,128)(2,1)} %copy.37), calls=%async_computation.1 | async-start | bytes 327680 | tf_op jit(solution)/shard_map/all_to_all | solution.py:60
  470.6 306.3 %copy-start.1 = (bf16[1,256,4096]{2,1,0:T(8,128)(2,1)S(1)}, bf16[1,256,4096]{2,1,0:T(8,128)(2,1)}, u32[]{:S(2)}) copy-start(bf16[1,256,4096]{2,1,0:T(8,128)(2,1)} %param.12) | copy-start | bytes 6291460
  693.7 81.9 %all-to-all-start.3 = ((bf16[8,80,128]{2,1,0:T(8,128)(2,1)}), bf16[8,80,128]{2,1,0:T(8,128)(2,1)S(1)}, u32[]{:S(2)}, u32[]{:S(2)}) async-start(bf16[8,80,128]{2,1,0:T(8,128)(2,1)} %copy.39), calls=%async_computation.3 | async-start | bytes 327680 | tf_op jit(solution)/shard_map/all_to_all | solution.py:60
Sparse Core Ops, SparseCore 0:
  26.1 88.9 all-gather.2
  117.6 87.0 all-gather.4
  238.4 225.3 reduce-scatter.6
  467.6 224.0 reduce-scatter.8
where the time goes:
time: 785 us; the launch traced here: 783 us
  waiting for transfers between devices  555 us (71%)
  blocking collectives  92.6 us (12%)
  local copies, waits for them, and re-layouts  62.1 us (8%)
  matrix products  45.3 us (6%)
  between operations  14 us (2%)
  starting transfers between devices  9.93 us (1%)
    unnamed x6, waiting for transfers between devices  396 us
    all_gather x2, waiting for transfers between devices, to_experts(): whole = lax.all_gather(arrived, 'section', axis=2, tiled=True)  159 us
    psum x1, blocking collectives, per_device(): grad_mix = lax.psum(mix_terms, 'section')  72.8 us
    unnamed x31, local copies, waits for them, and re-layouts  55.6 us
    all_to_all x2, blocking collectives, to_experts(): lax.all_to_all(block.reshape(experts, capacity, -1), 'expert', split_axis...  19.8 us
  transfers between devices with their start and end apart: 6, of which 4 were waited for; matrix products, arithmetic and copies ran while one was open for 9% of the time, Pallas kernels for 0%

commit v1 on v0

--- a/solution.py
+++ b/solution.py
@@ -2,6 +2,7 @@
 import jax.numpy as jnp
 from jax import lax
 from jax.sharding import PartitionSpec as P
+from jax.lax import axis_size, ppermute
 
 highest = lax.Precision.HIGHEST
 
@@ -73,7 +74,19 @@
     picked = returned[target]
     upstream_wide = upstream.astype(jnp.float32)
     mix_terms = jnp.einsum("tkd,td->tk", picked, upstream_wide, precision=highest)
-    grad_mix = lax.psum(mix_terms, "section")
+
+    def register_ways_up(link_axis, local_block):
+        n_chips = axis_size(link_axis)
+        known = local_block
+        for no in [ii for ii in (1, 2, 4, 8, 16) if ii < n_chips]:
+            known = known + ppermute(
+                known,
+                axis_name=link_axis,
+                perm=[(hop_no, hop_no ^ no) for hop_no in range(n_chips)],
+            )
+        return known
+
+    grad_mix = register_ways_up("section", mix_terms)
     grad_rows = to_experts(upstream, slot_scale)
     grad_hidden = lax.dot_general(
         grad_rows, down_local, (((1,), (1,)), ((), ())), preferred_element_type=jnp.float32

time: 785 us -> 716 us (0.912)
  blocking collectives: 92.6 us -> 19.8 us
  starting transfers between devices: 9.93 us -> 18.8 us
    psum x1 -> x0, blocking collectives: 72.8 us -> none  [per_device(): grad_mix = lax.psum(mix_terms, 'section')]
    ppermute x0 -> x5, starting transfers between devices: none -> 8.81 us  [register_ways_up(): ppermute(known, axis_name=link_axis, perm=[(hop_no, hop_no ^ no) for hop_...]
    unnamed x31 -> x39, local copies, waits for them, and re-layouts: 55.6 us -> 55 us
  transfers between devices with their start and end apart: 6 -> 11, of which waited for: 4 -> 7; matrix products, arithmetic and copies ran while one was open for 9% -> 9% of each run, Pallas kernels for 0% -> 0%
where the time goes in v1:
time: 716 us; the launch traced here: 714 us
  waiting for transfers between devices  554 us (77%)
  local copies, waits for them, and re-layouts  61.5 us (9%)
  matrix products  40.4 us (6%)
  blocking collectives  19.8 us (3%)
  starting transfers between devices  18.8 us (3%)
  between operations  14 us (2%)
    unnamed x6, waiting for transfers between devices  389 us
    all_gather x2, waiting for transfers between devices, to_experts(): whole = lax.all_gather(arrived, 'section', axis=2, tiled=True)  159 us
    unnamed x39, local copies, waits for them, and re-layouts  55 us
    all_to_all x2, blocking collectives, to_experts(): lax.all_to_all(block.reshape(experts, capacity, -1), 'expert', split_axis...  19.8 us
  transfers between devices with their start and end apart: 11, of which 7 were waited for; matrix products, arithmetic and copies ran while one was open for 9% of the time, Pallas kernels for 0%

profile of v1, /device:TPU:8, one launch (start us, length us, event | category | flops | bytes accessed | tf_op | source)
XLA Modules:
  0.0 714.2 jit_solution(3954726751920810985)
XLA Ops:
  15.7 10.3 %all_to_all.20 = bf16[8,80,128]{2,1,0:T(8,128)(2,1)} all-to-all(bf16[8,80,128]{2,1,0:T(8,128)(2,1)S(1)} %fusion.17), channel_id=1, replica_groups=mesh['section'=32,'expert'=8] {'expert'}, dimensions={0} | all-to-all | bytes 327680 | tf_op jit(solution)/shard_map/all_to_all | solution.py:48
  28.3 9.6 %all_to_all.21 = bf16[8,80,128]{2,1,0:T(8,128)(2,1)} all-to-all(bf16[8,80,128]{2,1,0:T(8,128)(2,1)S(1)} %fusion.16), channel_id=1, replica_groups=mesh['section'=32,'expert'=8] {'expert'}, dimensions={0} | all-to-all | bytes 327680 | tf_op jit(solution)/shard_map/all_to_all | solution.py:48
  37.9 77.2 %all-gather.3.cloned.1.call-done = bf16[8,80,4096]{2,1,0:T(8,128)(2,1)} async-done(((bf16[8,80,128]{2,1,0:T(8,128)(2,1)}), bf16[8,80,4096]{2,1,0:T(8,128)(2,1)}) %all-gather.3.cloned.1.call-update) | async-done | bytes 5242896 | tf_op jit(solution)/shard_map/all_gather | solution.py:51
  115.1 5.7 fusion.7
  123.2 81.6 %all-gather.5.cloned.1.call-done = bf16[8,80,4096]{2,1,0:T(8,128)(2,1)} async-done(((bf16[8,80,128]{2,1,0:T(8,128)(2,1)}), bf16[8,80,4096]{2,1,0:T(8,128)(2,1)}) %all-gather.5.cloned.1.call-update) | async-done | bytes 5242896 | tf_op jit(solution)/shard_map/all_gather | solution.py:51
  204.7 5.4 multiply_convert_fusion
  210.1 3.8 convolution_convert_fusion
  213.9 11.2 %copy.36 = bf16[8,80,4096]{1,0,2:T(8,128)(2,1)} copy(bf16[8,80,4096]{2,1,0:T(8,128)(2,1)} %convolution_convert_fusion) | data formatting | bytes 10485760
  225.1 13.1 %reshape.124 = bf16[4096,640]{1,0:T(8,128)(2,1)} reshape(bf16[4096,8,80]{2,1,0:T(8,128)(2,1)} %bitcast.67) | data formatting | bytes 10485760
  239.8 2.7 fusion.9
  242.5 3.8 add_convert_fusion
  246.4 11.2 %copy.38 = bf16[8,80,4096]{1,0,2:T(8,128)(2,1)} copy(bf16[8,80,4096]{2,1,0:T(8,128)(2,1)} %bitcast.70) | data formatting | bytes 10485760
  257.5 13.1 %reshape.126 = bf16[4096,640]{1,0:T(8,128)(2,1)} reshape(bf16[4096,8,80]{2,1,0:T(8,128)(2,1)} %bitcast.68) | data formatting | bytes 10485760
  270.7 193.2 %reduce-scatter.7.cloned.1.call-done = bf16[128,640]{1,0:T(8,128)(2,1)} async-done(((bf16[4096,640]{1,0:T(8,128)(2,1)}), bf16[128,640]{1,0:T(8,128)(2,1)}) %reduce-scatter.7.cloned.1.call-update) | async-done | bytes 163856
  465.9 4.8 all-to-all-start.1
  471.1 4.7 all-to-all-done.1
  478.3 6.0 fusion.1
  484.4 2.4 collective-permute-start.1
  486.7 3.2 fusion
  490.0 3.0 collective-permute-start.2
  493.0 3.2 fusion.2
  496.2 195.3 %reduce-scatter.9.cloned.1.call-done = bf16[128,640]{1,0:T(8,128)(2,1)} async-done(((bf16[4096,640]{1,0:T(8,128)(2,1)}), bf16[128,640]{1,0:T(8,128)(2,1)}) %reduce-scatter.9.cloned.1.call-update) | async-done | bytes 163856
  693.5 4.8 all-to-all-start.3
  699.0 2.4 fusion.13
  (89 shorter events, 28.5 us)
Async XLA Ops:
  7.2 197.6 %copy-start = (bf16[1,256,4096]{2,1,0:T(8,128)(2,1)S(1)}, bf16[1,256,4096]{2,1,0:T(8,128)(2,1)}, u32[]{:S(2)}) copy-start(bf16[1,256,4096]{2,1,0:T(8,128)(2,1)} %param.12) | copy-start | bytes 6291460
  7.2 6.4 copy-start.2
  7.2 18.9 %copy-start.3 = (bf16[256,128]{1,0:T(8,128)(2,1)S(1)}, bf16[256,128]{1,0:T(8,128)(2,1)}, u32[]{:S(2)}) copy-start(bf16[256,128]{1,0:T(8,128)(2,1)} %param.13) | copy-start | bytes 196612
  7.2 107.9 %all-gather.3.cloned.1.call-start = ((), (), s32[]{:S(2)}) async-start(), calls=%async_computation.6 | async-start | bytes 5406720 | tf_op jit(solution)/shard_map/all_gather | solution.py:51
  26.0 178.7 %all-gather.5.cloned.1.call-start = ((), (), s32[]{:S(2)}) async-start(), calls=%async_computation.7 | async-start | bytes 5406720 | tf_op jit(solution)/shard_map/all_gather | solution.py:51
  37.9 426.0 %reduce-scatter.7.cloned.1.call-start = ((), (), s32[]{:S(2)}) async-start(), calls=%async_computation.8 | async-start | bytes 5406720
  115.1 5.7 copy-start.4
  115.1 5.7 copy-start.10
  238.2 453.2 %reduce-scatter.9.cloned.1.call-start = ((), (), s32[]{:S(2)}) async-start(), calls=%async_computation.9 | async-start | bytes 5406720
  239.8 2.7 copy-start.8
  270.6 207.7 %copy-start.9 = (bf16[640,256]{1,0:T(8,128)(2,1)S(1)}, bf16[640,256]{1,0:T(8,128)(2,1)}, u32[]{:S(2)}) copy-start(bf16[640,256]{1,0:T(8,128)(2,1)} %get-tuple-element.12) | copy-start | bytes 983044
  465.9 9.8 %all-to-all-start.1 = ((bf16[8,80,128]{2,1,0:T(8,128)(2,1)}), bf16[8,80,128]{2,1,0:T(8,128)(2,1)S(1)}, u32[]{:S(2)}, u32[]{:S(2)}) async-start(bf16[8,80,128]{2,1,0:T(8,128)(2,1)} %copy.37), calls=%async_computation.1 | async-start | bytes 327680 | tf_op jit(solution)/shard_map/all_to_all | solution.py:61
  477.6 9.1 %slice-start.2 = ((s8[5242880]{0:T(1024)(128)(4,1)}), s8[4194304]{0:T(1024)(128)(4,1)S(1)}, s32[]{:S(2)}) async-start(s8[5242880]{0:T(1024)(128)(4,1)} %bitcast.88), calls=%async_computation.12 | async-start | bytes 8388608
  477.6 9.1 %copy-start.7 = (bf16[640,256]{1,0:T(8,128)(2,1)S(1)}, bf16[640,256]{1,0:T(8,128)(2,1)}, u32[]{:S(2)}) copy-start(bf16[640,256]{1,0:T(8,128)(2,1)} %get-tuple-element.13) | copy-start | bytes 983044
  477.6 9.1 %slice-start.3 = ((s8[5242880]{0:T(1024)(128)(4,1)}), s8[1048576]{0:T(1024)(128)(4,1)S(1)}, s32[]{:S(2)}) async-start(s8[5242880]{0:T(1024)(128)(4,1)} %bitcast.88), calls=%async_computation.13 | async-start | bytes 2097152
  477.6 6.7 collective-permute-start
  484.3 8.6 %slice-start = ((s8[5242880]{0:T(1024)(128)(4,1)}), s8[4194304]{0:T(1024)(128)(4,1)S(1)}, s32[]{:S(2)}) async-start(s8[5242880]{0:T(1024)(128)(4,1)} %bitcast.72), calls=%async_computation.10 | async-start | bytes 8388608
  484.3 8.6 %slice-start.1 = ((s8[5242880]{0:T(1024)(128)(4,1)}), s8[1048576]{0:T(1024)(128)(4,1)S(1)}, s32[]{:S(2)}) async-start(s8[5242880]{0:T(1024)(128)(4,1)} %bitcast.72), calls=%async_computation.11 | async-start | bytes 2097152
  484.4 5.6 collective-permute-start.1
  490.0 208.3 %collective-permute-start.2 = (f32[256,2]{0,1:T(2,128)S(1)}, f32[256,2]{0,1:T(2,128)S(1)}, u32[]{:S(2)}, u32[]{:S(2)}) collective-permute-start(f32[256,2]{0,1:T(2,128)S(1)} %add.67), channel_id=1, source_target_pairs={{0,32},{8,40},{16,48},{24,56},{32,0},{40,8},{48,16},{56,24},{64,96... | collective-permute-start | bytes 6152 | tf_op jit(solution)/shard_map/ppermute | solution.py:82
  493.0 214.7 %copy-start.1 = (bf16[1,256,4096]{2,1,0:T(8,128)(2,1)S(1)}, bf16[1,256,4096]{2,1,0:T(8,128)(2,1)}, u32[]{:S(2)}) copy-start(bf16[1,256,4096]{2,1,0:T(8,128)(2,1)} %param.12) | copy-start | bytes 6291460
  693.5 10.6 %all-to-all-start.3 = ((bf16[8,80,128]{2,1,0:T(8,128)(2,1)}), bf16[8,80,128]{2,1,0:T(8,128)(2,1)S(1)}, u32[]{:S(2)}, u32[]{:S(2)}) async-start(bf16[8,80,128]{2,1,0:T(8,128)(2,1)} %copy.39), calls=%async_computation.3 | async-start | bytes 327680 | tf_op jit(solution)/shard_map/all_to_all | solution.py:61
  698.3 3.7 collective-permute-start.3
  702.0 5.1 collective-permute-start.4
  (2 other events, 4.3 us)
Sparse Core Ops, SparseCore 0:
  26.1 88.9 all-gather.2
  117.6 87.0 all-gather.4
  238.4 225.4 reduce-scatter.6
  467.7 223.7 reduce-scatter.8
